TPU v7x, 32 devices: a whole 2x2x4 slice. The times are simulated.
32 devices in a mesh: dp: 8 (over y, x, core), tensor: 4 (over z).
Axes of the slice: x: 2, y: 2, z: 4, core: 2. Of those that a mesh axis runs over, the one named last changes fastest.
Arguments:
- tokens: bfloat16 [4096, 1024], P('dp'), may hold values from -6 to 6
- segments: int32 [8, 512], P('dp'), may hold values from 0 to 1, never falling along the last dimension, each value on 1 to 384 neighbouring positions
- ln1_gain: float32 [1024], replicated, may hold values from 0.1 to 1.9
- ln1_bias: float32 [1024], replicated, may hold values from -3 to 3
- w_qkv: bfloat16 [1024, 3072], P(None, 'tensor'), may hold values from -0.2 to 0.2
- b_qv: float32 [16, 128], P('tensor'), may hold values from -3 to 3
- w_dense: bfloat16 [1024, 1024], P('tensor'), may hold values from -0.75 to 0.75
- b_dense: float32 [1024], replicated, may hold values from -3 to 3
- ln2_gain: float32 [1024], replicated, may hold values from 0.1 to 1.9
- ln2_bias: float32 [1024], replicated, may hold values from -3 to 3
- w_fc1: bfloat16 [1024, 4096], P(None, 'tensor'), may hold values from -0.1875 to 0.1875
- b_fc1: float32 [32, 128], P('tensor'), may hold values from -3 to 3
- w_fc2: bfloat16 [4096, 1024], P('tensor'), may hold values from -0.09375 to 0.09375
- b_fc2: float32 [1024], replicated, may hold values from -3 to 3
- cotangent: bfloat16 [4096, 1024], P('dp'), may hold values from -6 to 6
Outputs:
- block_out: bfloat16 [4096, 1024], P(('dp', 'tensor'))
- d_tokens: float32 [4096, 1024], P(('dp', 'tensor'))
- d_ln1_gain: float32 [1024], P(('dp', 'tensor'))
- d_ln1_bias: float32 [1024], P(('dp', 'tensor'))
- d_w_qkv: float32 [1024, 3072], P('dp', 'tensor')
- d_b_qv: float32 [16, 128], P('tensor', 'dp')
- d_w_dense: float32 [1024, 1024], P('tensor', 'dp')
- d_b_dense: float32 [1024], P(('dp', 'tensor'))
- d_ln2_gain: float32 [1024], P(('dp', 'tensor'))
- d_ln2_bias: float32 [1024], P(('dp', 'tensor'))
- d_w_fc1: float32 [1024, 4096], P('dp', 'tensor')
- d_b_fc1: float32 [32, 128], P('tensor', 'dp')
- d_w_fc2: float32 [4096, 1024], P('tensor', 'dp')
- d_b_fc2: float32 [1024], P(('dp', 'tensor'))
Inputs may be any that keep to these rules, and one draw needn't show every extreme that they name: `segments`: along each row the numbers never fall; positions with equal numbers form one document of at most 384 tokens.
All inputs are finite; a program needn't handle non-finite values.
Results may differ from a plain program's by a relative error of at most 0.034.
The roundings to bfloat16 on the way count: a program that leaves them out, or rounds other values in their place, can miss the bound.
Values may be sent and summed in bfloat16 or wider, within the bound.
A program may use at most 128 MiB of HBM per device.

v0:
```python
import math

import jax
import jax.numpy as jnp
from jax import lax
from jax.sharding import PartitionSpec as P

H = 16


EPS = 1e-05
GELU_C = 0.7978845608028654
GELU_A = 0.044715
MASKED = -1e30


def layer_norm(row_block, gain_row, shift_row):
    row_mean = jnp.mean(row_block, axis=-1, keepdims=True)
    centred = row_block - row_mean
    row_var = jnp.mean(centred * centred, axis=-1, keepdims=True)
    inv_std = lax.rsqrt(row_var + EPS)
    normed = centred * inv_std
    return (normed * gain_row + shift_row, normed, inv_std)


def norm_back(grad_rows, normed, inv_std, gain_row):
    grad_normed = grad_rows * gain_row
    mean_one = jnp.mean(grad_normed, axis=-1, keepdims=True)
    mean_two = jnp.mean(grad_normed * normed, axis=-1, keepdims=True)
    grad_in = inv_std * (grad_normed - mean_one - normed * mean_two)
    return (grad_in, jnp.sum(grad_rows * normed, axis=0), jnp.sum(grad_rows, axis=0))


def gelu_value(pre_act):
    tanh_val = jnp.tanh(GELU_C * (pre_act + GELU_A * pre_act * pre_act * pre_act))
    return 0.5 * pre_act * (1.0 + tanh_val)


def gelu_slope(pre_act):
    tanh_val = jnp.tanh(GELU_C * (pre_act + GELU_A * pre_act * pre_act * pre_act))
    return 0.5 * (1.0 + tanh_val) + 0.5 * pre_act * (1.0 - tanh_val * tanh_val) * GELU_C * (
        1.0 + 3.0 * GELU_A * pre_act * pre_act
    )


def alibi_slopes(head_ids, head_total):
    return jnp.power(2.0, -8.0 * (head_ids.astype(jnp.float32) + 1.0) / head_total)


def qkv_bias(bias_table):
    head_size = bias_table.shape[1] // 2
    zero_keys = jnp.zeros((bias_table.shape[0], head_size), jnp.float32)
    return jnp.concatenate(
        [bias_table[:, :head_size], zero_keys, bias_table[:, head_size:]], axis=1
    ).reshape(-1)


def cross_rows(left_mat, right_mat):
    return lax.dot_general(
        left_mat, right_mat, (((0,), (0,)), ((), ())), preferred_element_type=jnp.float32
    )


def dot_transposed(left_mat, right_mat):
    return lax.dot_general(
        left_mat, right_mat, (((1,), (1,)), ((), ())), preferred_element_type=jnp.float32
    )


def masked_scores(queries, keys_all, slopes, doc_ids, head_size):
    raw_dot = jnp.einsum("qhe,khe->hqk", queries, keys_all, preferred_element_type=jnp.float32)
    places = jnp.arange(doc_ids.shape[0])
    distance = (places[:, None] - places[None, :]).astype(jnp.float32)
    allowed = jnp.logical_and(
        doc_ids[:, None] == doc_ids[None, :], places[None, :] <= places[:, None]
    )
    scores = raw_dot * (1.0 / math.sqrt(head_size)) - slopes[:, None, None] * distance[None]
    return jnp.where(allowed[None], scores, MASKED)


def local(
    tokens,
    segments,
    ln1_gain,
    ln1_bias,
    w_qkv,
    b_qv,
    w_dense,
    b_dense,
    ln2_gain,
    ln2_bias,
    w_fc1,
    b_fc1,
    w_fc2,
    b_fc2,
    cotangent,
):
    tensor_count = lax.axis_size("tensor")
    tensor_rank = lax.axis_index("tensor")
    length = tokens.shape[0]
    share_rows = length // tensor_count
    head_count = b_qv.shape[0]
    head_size = b_qv.shape[1] // 2
    offset = tensor_rank * share_rows
    doc_ids = segments[0]
    tokens_f = tokens.astype(jnp.float32)
    norm_one, normed_one, inv_one = layer_norm(tokens_f, ln1_gain, ln1_bias)
    input_one = norm_one.astype(jnp.bfloat16)
    qkv_rows = (
        jnp.dot(input_one, w_qkv, preferred_element_type=jnp.float32) + qkv_bias(b_qv)
    ).astype(jnp.bfloat16)
    qkv_rows = qkv_rows.reshape(length, head_count, 3, head_size)
    queries = qkv_rows[:, :, 0]
    keys_all = qkv_rows[:, :, 1]
    values_all = qkv_rows[:, :, 2]
    slopes = alibi_slopes(tensor_rank * head_count + jnp.arange(head_count), H)
    scores = masked_scores(queries, keys_all, slopes, doc_ids, head_size)
    row_max = jnp.max(scores, axis=-1, keepdims=True)
    log_total = row_max + jnp.log(jnp.sum(jnp.exp(scores - row_max), axis=-1, keepdims=True))
    attn_probs = jnp.exp(scores - log_total).astype(jnp.bfloat16)
    context = jnp.einsum("hqk,khe->qhe", attn_probs, values_all, preferred_element_type=jnp.float32)
    context = context.astype(jnp.bfloat16).reshape(length, head_count * head_size)
    attn_share = lax.psum_scatter(
        jnp.dot(context, w_dense, preferred_element_type=jnp.float32),
        "tensor",
        scatter_dimension=0,
        tiled=True,
    )
    tokens_share = lax.dynamic_slice_in_dim(tokens_f, offset, share_rows, 0)
    resid_one = tokens_share + attn_share + b_dense
    norm_two, normed_two, inv_two = layer_norm(resid_one, ln2_gain, ln2_bias)
    input_two = lax.all_gather(norm_two.astype(jnp.bfloat16), "tensor", axis=0, tiled=True)
    pre_act = jnp.dot(input_two, w_fc1, preferred_element_type=jnp.float32) + b_fc1.reshape(-1)
    hidden = gelu_value(pre_act).astype(jnp.bfloat16)
    mlp_share = lax.psum_scatter(
        jnp.dot(hidden, w_fc2, preferred_element_type=jnp.float32).astype(jnp.bfloat16),
        "tensor",
        scatter_dimension=0,
        tiled=True,
    ).astype(jnp.float32)
    block_out = (resid_one + mlp_share + b_fc2).astype(jnp.bfloat16)
    grad_share = lax.dynamic_slice_in_dim(cotangent, offset, share_rows, 0).astype(jnp.float32)
    g_b_fc2 = jnp.sum(grad_share, axis=0)
    g_w_fc2 = cross_rows(hidden, cotangent)
    grad_pre = dot_transposed(cotangent, w_fc2) * gelu_slope(pre_act)
    g_b_fc1 = jnp.sum(grad_pre, axis=0).reshape(b_fc1.shape)
    grad_pre_b = grad_pre.astype(jnp.bfloat16)
    g_w_fc1 = cross_rows(input_two, grad_pre_b)
    grad_two = lax.psum_scatter(
        dot_transposed(grad_pre_b, w_fc1), "tensor", scatter_dimension=0, tiled=True
    )
    grad_ln_two, g_ln2_gain, g_ln2_bias = norm_back(grad_two, normed_two, inv_two, ln2_gain)
    grad_resid = grad_share + grad_ln_two
    g_b_dense = jnp.sum(grad_resid, axis=0)
    grad_resid_b = lax.all_gather(grad_resid.astype(jnp.bfloat16), "tensor", axis=0, tiled=True)
    g_w_dense = cross_rows(context, grad_resid_b)
    grad_context = dot_transposed(grad_resid_b, w_dense).reshape(length, head_count, head_size)
    delta = jnp.einsum(
        "qhe,qhe->hq",
        grad_context,
        context.reshape(length, head_count, head_size).astype(jnp.float32),
    )
    grad_context_b = grad_context.astype(jnp.bfloat16)
    grad_probs = jnp.einsum(
        "qhe,khe->hqk", grad_context_b, values_all, preferred_element_type=jnp.float32
    )
    again_scores = masked_scores(queries, keys_all, slopes, doc_ids, head_size)
    prob_full = jnp.exp(again_scores - log_total)
    again_probs = prob_full.astype(jnp.bfloat16)
    grad_scores = (prob_full * (grad_probs - delta[:, :, None])).astype(jnp.bfloat16)
    inv_root = 1.0 / math.sqrt(head_size)
    grad_q = (
        jnp.einsum("hqk,khe->qhe", grad_scores, keys_all, preferred_element_type=jnp.float32)
        * inv_root
    )
    grad_k = (
        jnp.einsum("hqk,qhe->khe", grad_scores, queries, preferred_element_type=jnp.float32)
        * inv_root
    )
    grad_v = jnp.einsum(
        "hqk,qhe->khe", again_probs, grad_context_b, preferred_element_type=jnp.float32
    )
    g_b_qv = jnp.concatenate([jnp.sum(grad_q, axis=0), jnp.sum(grad_v, axis=0)], axis=-1)
    grad_qkv = (
        jnp.stack([grad_q, grad_k, grad_v], axis=2)
        .astype(jnp.bfloat16)
        .reshape(length, 3 * head_count * head_size)
    )
    g_w_qkv = cross_rows(input_one, grad_qkv)
    grad_one = lax.psum_scatter(
        dot_transposed(grad_qkv, w_qkv).astype(jnp.bfloat16),
        "tensor",
        scatter_dimension=0,
        tiled=True,
    ).astype(jnp.float32)
    normed_share = lax.dynamic_slice_in_dim(normed_one, offset, share_rows, 0)
    inv_share = lax.dynamic_slice_in_dim(inv_one, offset, share_rows, 0)
    grad_ln_one, g_ln1_gain, g_ln1_bias = norm_back(grad_one, normed_share, inv_share, ln1_gain)
    d_tokens = grad_resid + grad_ln_one
    sent_qkv, sent_qv, sent_dense, sent_fc1, sent_bias, sent_fc2 = (
        lax.psum_scatter(g_w_qkv, "dp", scatter_dimension=0, tiled=True),
        lax.psum_scatter(g_b_qv, "dp", scatter_dimension=1, tiled=True),
        lax.psum_scatter(g_w_dense, "dp", scatter_dimension=1, tiled=True),
        lax.psum_scatter(g_w_fc1, "dp", scatter_dimension=0, tiled=True),
        lax.psum_scatter(g_b_fc1, "dp", scatter_dimension=1, tiled=True),
        lax.psum_scatter(g_w_fc2, "dp", scatter_dimension=1, tiled=True),
    )
    small_sums = (
        lax.psum_scatter(g_ln1_gain, ("dp", "tensor"), scatter_dimension=0, tiled=True),
        lax.psum_scatter(g_ln1_bias, ("dp", "tensor"), scatter_dimension=0, tiled=True),
        lax.psum_scatter(g_b_dense, ("dp", "tensor"), scatter_dimension=0, tiled=True),
        lax.psum_scatter(g_ln2_gain, ("dp", "tensor"), scatter_dimension=0, tiled=True),
        lax.psum_scatter(g_ln2_bias, ("dp", "tensor"), scatter_dimension=0, tiled=True),
        lax.psum_scatter(g_b_fc2, ("dp", "tensor"), scatter_dimension=0, tiled=True),
    )
    return (
        block_out,
        d_tokens,
        small_sums[0],
        small_sums[1],
        sent_qkv,
        sent_qv,
        sent_dense,
        small_sums[2],
        small_sums[3],
        small_sums[4],
        sent_fc1,
        sent_bias,
        sent_fc2,
        small_sums[5],
    )


def solution(mesh):
    placed = (
        P("dp", None),
        P("dp", None),
        P(),
        P(),
        P(None, "tensor"),
        P("tensor", None),
        P("tensor", None),
        P(),
        P(),
        P(),
        P(None, "tensor"),
        P("tensor", None),
        P("tensor", None),
        P(),
        P("dp", None),
    )
    return jax.shard_map(
        local,
        mesh=mesh,
        in_specs=placed,
        out_specs=(
            P(("dp", "tensor"), None),
            P(("dp", "tensor"), None),
            P(("dp", "tensor")),
            P(("dp", "tensor")),
            P("dp", "tensor"),
            P("tensor", "dp"),
            P("tensor", "dp"),
            P(("dp", "tensor")),
            P(("dp", "tensor")),
            P(("dp", "tensor")),
            P("dp", "tensor"),
            P("tensor", "dp"),
            P("tensor", "dp"),
            P(("dp", "tensor")),
        ),
        check_vma=False,
    )
```

profile of v0, /device:TPU:0, one launch (start us, length us, event | category | flops | bytes accessed | tf_op | source)
XLA Modules:
  0.0 520.9 jit_solution(12540974133909188816)
XLA Ops:
  7.3 1.1 subtract_convert_fusion
  8.4 1.5 convert_reduce_fusion
  9.9 0.4 multiply_reduce_fusion
  10.6 3.5 add_convert_fusion.1
  14.1 2.3 copy.47
  16.6 2.7 fusion.34
  19.3 0.6 exponential_reduce_fusion
  19.9 1.3 copy-done.1
  21.2 1.8 convolution_convert_fusion.2
  23.0 1.8 fusion.36
  25.0 1.6 convert_element_type.76
  26.5 44.8 %reduce-scatter.15.cloned.1.call-done = f32[128,1024]{1,0:T(8,128)} async-done(((f32[512,1024]{1,0:T(8,128)}), f32[128,1024]{1,0:T(8,128)}) %reduce-scatter.15.cloned.1.call-update) | async-done | bytes 524304 | tf_op jit(solution)/shard_map/reduce_scatter | solution.py:123
  71.4 1.3 fusion.30
  72.9 0.6 copy-done.4
  73.5 0.9 add_convert_fusion.3
  74.5 27.3 %all-gather.3.cloned.1.call-done = bf16[512,1024]{1,0:T(8,128)(2,1)} async-done(((bf16[128,1024]{1,0:T(8,128)(2,1)}), bf16[512,1024]{1,0:T(8,128)(2,1)}) %all-gather.3.cloned.1.call-update) | async-done | bytes 1048592 | tf_op jit(solution)/shard_map/all_gather | solution.py:132
  101.7 3.2 fusion.37
  105.0 2.4 fusion.35
  107.5 1.0 copy-done.7
  108.5 2.6 fusion.23
  111.2 4.1 convolution_convert_fusion.1
  115.3 0.2 all-gather.5.cloned.1.call-start
  115.5 38.8 %reduce-scatter.19.cloned.1.call-done = f32[128,1024]{1,0:T(8,128)} async-done(((f32[512,1024]{1,0:T(8,128)}), f32[128,1024]{1,0:T(8,128)}) %reduce-scatter.19.cloned.1.call-update) | async-done | bytes 524304 | tf_op jit(solution)/shard_map/reduce_scatter | solution.py:149
  154.3 1.5 multiply_reduce_fusion.2
  155.8 27.2 %reduce-scatter.17.cloned.1.call-done = bf16[128,1024]{1,0:T(8,128)(2,1)} async-done(((bf16[512,1024]{1,0:T(8,128)(2,1)}), bf16[128,1024]{1,0:T(8,128)(2,1)}) %reduce-scatter.17.cloned.1.call-update) | async-done | bytes 262160 | tf_op jit(solution)/shard_map/reduce_scatter | solution.py:135
  182.9 2.3 fusion.29
  185.3 0.8 copy-done.5
  186.0 0.7 convert_element_type.91
  186.9 0.7 copy.70
  187.6 25.8 %all-gather.5.cloned.1.call-done = bf16[512,1024]{1,0:T(8,128)(2,1)} async-done(((bf16[128,1024]{1,0:T(8,128)(2,1)}), bf16[512,1024]{1,0:T(8,128)(2,1)}) %all-gather.5.cloned.1.call-update) | async-done | bytes 1048592 | tf_op jit(solution)/shard_map/all_gather | solution.py:155
  213.4 1.8 multiply_reduce_fusion.1
  215.3 3.1 convolution_bitcast_fusion
  218.4 0.3 copy-done.2
  218.7 0.2 copy-done.6
  218.9 1.0 multiply_convert_fusion
  220.0 0.8 fusion.9
  220.7 0.6 fusion.31
  221.3 1.0 pad_maximum_fusion
  222.4 0.7 copy.68
  223.1 2.1 copy.56
  225.2 3.7 convolution_convert_fusion
  229.0 4.8 fusion.21
  233.8 5.4 %fusion.28 = f32[1024,1024]{1,0:T(8,128)} fusion(bf16[512,1024]{1,0:T(8,128)(2,1)} %param.29, f32[512,1024]{1,0:T(8,128)} %copy-done.20, f32[1024]{0:T(1024)S(1)} %bitcast.100), kind=kOutput, calls=%fused_computation.78 | convolution fusion | flops 1078984704 | bytes 7344128 | tf_op jit(solution)/shard_map/dot_general | solution.py:59
  239.3 2.6 fusion.38
  242.0 4.1 fusion.25
  246.3 1.7 subtract_multiply_fusion
  248.0 1.2 reduce-scatter.33.cloned.1.call-done
  249.2 1.4 copy.71
  250.6 35.2 %reduce-scatter.31.cloned.1.call-done = f32[16,4]{1,0:T(8,128)} async-done(((f32[128,4]{1,0:T(8,128)}), f32[16,4]{1,0:T(8,128)}) %reduce-scatter.31.cloned.1.call-update) | async-done | bytes 272
  285.8 1.3 copy.69
  287.1 28.2 %reduce-scatter.21.cloned.1.call-done = bf16[128,1024]{1,0:T(8,128)(2,1)} async-done(((bf16[512,1024]{1,0:T(8,128)(2,1)}), bf16[128,1024]{1,0:T(8,128)(2,1)}) %reduce-scatter.21.cloned.1.call-update) | async-done | bytes 262160 | tf_op jit(solution)/shard_map/reduce_scatter | solution.py:190
  315.3 1.3 fusion.20
  316.7 39.4 %all-reduce.6 = (f32[1024]{0:T(1024)S(1)}, f32[1024]{0:T(1024)S(1)}, f32[1024]{0:T(1024)S(1)}, f32[1024]{0:T(1024)S(1)}, f32[1024]{0:T(1024)S(1)}, /*index=5*/f32[1024]{0:T(1024)S(1)}) all-reduce(f32[1024]{0:T(1024)S(1)} %get-tuple-element.14, ...), channel_id=6, replica_groups=mesh['dp'=8,'tensor'=4] {'dp','tensor'}, use_global_device_ids=true, to_apply=%region_15.16.clone | all-reduce | flops 6144 | bytes 49152
  356.1 0.6 dynamic-slice.4
  356.7 0.6 dynamic-slice.5
  357.3 0.6 dynamic-slice.6
  357.8 0.6 dynamic-slice.7
  358.4 0.6 dynamic-slice.8
  359.0 0.6 dynamic-slice.9
  359.6 2.5 fusion.18
  362.1 7.5 %reduce-scatter.27.cloned.1.call-done = f32[128,1024]{1,0:T(8,128)} async-done(((f32[1024,1024]{1,0:T(8,128)}), f32[128,1024]{1,0:T(8,128)}) %reduce-scatter.27.cloned.1.call-update) | async-done | bytes 524304 | tf_op jit(solution)/shard_map/reduce_scatter | solution.py:204
  369.5 54.9 %reduce-scatter.29.cloned.1.call-done = f32[1024,128]{1,0:T(8,128)} async-done(((f32[1024,1024]{1,0:T(8,128)}), f32[1024,128]{1,0:T(8,128)}) %reduce-scatter.29.cloned.1.call-update) | async-done | bytes 524304 | tf_op jit(solution)/shard_map/reduce_scatter | solution.py:206
  424.4 39.7 %reduce-scatter.25.cloned.1.call-done = f32[256,128]{1,0:T(8,128)} async-done(((f32[256,1024]{1,0:T(8,128)}), f32[256,128]{1,0:T(8,128)}) %reduce-scatter.25.cloned.1.call-update) | async-done | bytes 131088 | tf_op jit(solution)/shard_map/reduce_scatter | solution.py:203
  464.1 49.9 %reduce-scatter.23.cloned.1.call-done = f32[128,768]{1,0:T(8,128)} async-done(((f32[1024,768]{1,0:T(8,128)}), f32[128,768]{1,0:T(8,128)}) %reduce-scatter.23.cloned.1.call-update) | async-done | bytes 393232 | tf_op jit(solution)/shard_map/reduce_scatter | solution.py:201
  (78 shorter events, 1.6 us)
Async XLA Ops:
  7.2 97.8 %copy-start = (bf16[1024,1024]{1,0:T(8,128)(2,1)S(1)}, bf16[1024,1024]{1,0:T(8,128)(2,1)}, u32[]{:S(2)}) copy-start(bf16[1024,1024]{1,0:T(8,128)(2,1)} %param.27) | copy-start | bytes 6291460
  7.2 2.7 copy-start.3
  7.2 3.1 copy-start.13
  7.2 3.4 copy-start.11
  7.2 3.3 copy-start.19
  7.2 64.1 %reduce-scatter.15.cloned.1.call-start = ((), (), s32[]{:S(2)}) async-start(), calls=%async_computation.10 | async-start | bytes 2621440 | tf_op jit(solution)/shard_map/reduce_scatter | solution.py:123
  10.6 5.8 %copy-start.12 = (s32[1,512]{1,0:T(1,128)S(1)}, s32[1,512]{1,0:T(1,128)}, u32[]{:S(2)}) copy-start(s32[1,512]{1,0:T(1,128)} %param.16) | copy-start | bytes 6148
  19.3 1.9 copy-start.1
  21.2 1.8 copy-start.8
  24.9 46.5 %copy-start.14 = (f32[1024]{0:T(1024)S(1)}, f32[1024]{0:T(1024)}, u32[]{:S(2)}) copy-start(f32[1024]{0:T(1024)} %param.22) | copy-start | bytes 12292
  24.9 48.6 %copy-start.10 = (f32[1024]{0:T(1024)S(1)}, f32[1024]{0:T(1024)}, u32[]{:S(2)}) copy-start(f32[1024]{0:T(1024)} %param.23) | copy-start | bytes 12292
  24.9 48.6 %copy-start.15 = (f32[1024]{0:T(1024)S(1)}, f32[1024]{0:T(1024)}, u32[]{:S(2)}) copy-start(f32[1024]{0:T(1024)} %param.24) | copy-start | bytes 12292
  24.9 76.8 %all-gather.3.cloned.1.call-start = ((), (), s32[]{:S(2)}) async-start(), calls=%async_computation.11 | async-start | bytes 1310720 | tf_op jit(solution)/shard_map/all_gather | solution.py:132
  72.7 0.8 copy-start.4
  74.4 30.6 %copy-start.18 = (f32[8,128]{1,0:T(8,128)S(1)}, f32[8,128]{1,0:T(8,128)}, u32[]{:S(2)}) copy-start(f32[8,128]{1,0:T(8,128)} %param.26) | copy-start | bytes 12292
  74.4 79.9 %reduce-scatter.19.cloned.1.call-start = ((), (), s32[]{:S(2)}) async-start(), calls=%async_computation.13 | async-start | bytes 2621440 | tf_op jit(solution)/shard_map/reduce_scatter | solution.py:149
  101.7 3.3 copy-start.9
  105.0 2.5 copy-start.20
  105.0 3.4 copy-start.17
  107.5 1.0 copy-start.7
  111.1 71.8 %reduce-scatter.17.cloned.1.call-start = ((), (), s32[]{:S(2)}) async-start(), calls=%async_computation.12 | async-start | bytes 1310720 | tf_op jit(solution)/shard_map/reduce_scatter | solution.py:135
  115.2 67.7 %copy-start.16 = (f32[1024]{0:T(1024)S(1)}, f32[1024]{0:T(1024)}, u32[]{:S(2)}) copy-start(f32[1024]{0:T(1024)} %param.28) | copy-start | bytes 12292
  115.3 98.2 %all-gather.5.cloned.1.call-start = ((), (), s32[]{:S(2)}) async-start(), calls=%async_computation.14 | async-start | bytes 1310720 | tf_op jit(solution)/shard_map/all_gather | solution.py:155
  185.3 0.8 copy-start.5
  186.8 62.4 %reduce-scatter.33.cloned.1.call-start = ((), (), s32[]{:S(2)}) async-start(), calls=%async_computation.21 | async-start | bytes 73728
  187.6 98.2 %reduce-scatter.31.cloned.1.call-start = ((), (), s32[]{:S(2)}) async-start(), calls=%async_computation.20 | async-start | bytes 73728
  215.3 3.5 copy-start.2
  215.3 3.6 copy-start.6
  225.2 90.2 %reduce-scatter.21.cloned.1.call-start = ((), (), s32[]{:S(2)}) async-start(), calls=%async_computation.15 | async-start | bytes 1310720 | tf_op jit(solution)/shard_map/reduce_scatter | solution.py:190
  228.9 140.6 %reduce-scatter.27.cloned.1.call-start = ((), (), s32[]{:S(2)}) async-start(), calls=%async_computation.18 | async-start | bytes 4718592 | tf_op jit(solution)/shard_map/reduce_scatter | solution.py:204
  233.8 190.6 %reduce-scatter.29.cloned.1.call-start = ((), (), s32[]{:S(2)}) async-start(), calls=%async_computation.19 | async-start | bytes 4718592 | tf_op jit(solution)/shard_map/reduce_scatter | solution.py:206
  239.3 224.9 %reduce-scatter.25.cloned.1.call-start = ((), (), s32[]{:S(2)}) async-start(), calls=%async_computation.17 | async-start | bytes 1179648 | tf_op jit(solution)/shard_map/reduce_scatter | solution.py:203
  242.0 272.1 %reduce-scatter.23.cloned.1.call-start = ((), (), s32[]{:S(2)}) async-start(), calls=%async_computation.16 | async-start | bytes 3538944 | tf_op jit(solution)/shard_map/reduce_scatter | solution.py:201
Sparse Core Ops, SparseCore 0:
  25.0 46.3 reduce-scatter.14
  74.5 27.1 all-gather.2
  111.2 43.0 reduce-scatter.18
  156.4 26.4 reduce-scatter.16
  186.9 26.4 all-gather.4
  216.3 32.8 reduce-scatter.32
  252.2 33.5 reduce-scatter.30
  288.0 27.2 reduce-scatter.20
  319.3 50.2 reduce-scatter.26
  373.3 51.0 reduce-scatter.28
  428.2 35.9 reduce-scatter.24
  467.9 46.0 reduce-scatter.22
where the time goes:
time: 522 us; the launch traced here: 521 us
  waiting for transfers between devices  381 us (73%)
  matrix products  50.1 us (10%)
  blocking collectives  39.4 us (8%)
  other arithmetic  18.9 us (4%)
  local copies, waits for them, and re-layouts  16.6 us (3%)
  between operations  14.5 us (3%)
    reduce_scatter x1, waiting for transfers between devices, local(): lax.psum_scatter(g_w_fc2, 'dp', scatter_dimension=1, tiled=True)  54.9 us
    reduce_scatter x1, waiting for transfers between devices, local(): lax.psum_scatter(g_w_qkv, 'dp', scatter_dimension=0, tiled=True)  49.9 us
    reduce_scatter x1, waiting for transfers between devices, local(): lax.psum_scatter(jnp.dot(context, w_dense, preferred_element_type=jnp.flo...  44.8 us
    reduce_scatter x1, waiting for transfers between devices, local(): lax.psum_scatter(g_w_dense, 'dp', scatter_dimension=1, tiled=True)  39.7 us
    unnamed x1, blocking collectives  39.4 us
    reduce_scatter x1, waiting for transfers between devices, local(): lax.psum_scatter(dot_transposed(grad_pre_b, w_fc1), 'tensor', scatter_dim...  38.8 us
    unnamed x14, waiting for transfers between devices  36.6 us
    reduce_scatter x1, waiting for transfers between devices, local(): lax.psum_scatter(dot_transposed(grad_qkv, w_qkv).astype(jnp.bfloat16), 't...  28.2 us
  transfers between devices with their start and end apart: 12, of which 12 were waited for; matrix products, arithmetic and copies ran while one was open for 10% of the time, Pallas kernels for 0%

commit v1 on v0

--- a/solution.py
+++ b/solution.py
@@ -1,8 +1,11 @@
+import functools
 import math
 
 import jax
 import jax.numpy as jnp
 from jax import lax
+from jax.experimental import pallas as pl
+from jax.experimental.pallas import tpu as pltpu
 from jax.sharding import PartitionSpec as P
 
 H = 16
@@ -76,6 +79,311 @@
     )
     scores = raw_dot * (1.0 / math.sqrt(head_size)) - slopes[:, None, None] * distance[None]
     return jnp.where(allowed[None], scores, MASKED)
+
+
+PIECES = 4
+
+
+def greet(count, me):
+    barrier = pltpu.get_barrier_semaphore()
+    for step in range(1, count):
+        pl.semaphore_signal(
+            barrier,
+            inc=1,
+            device_id={"tensor": lax.rem(me + step, count)},
+            device_id_type=pl.DeviceIdType.MESH,
+        )
+    pl.semaphore_wait(barrier, count - 1)
+
+
+class Line:
+    def __init__(self, count, me, rows, share, stage, landed, sent_sem, got_sem):
+        self.count, self.me, self.rows = count, me, rows
+        self.size = rows // PIECES
+        self.share, self.stage, self.landed = share, stage, landed
+        self.sent_sem, self.got_sem = sent_sem, got_sem
+
+    def at(self, piece, chunk):
+        return pl.ds(pl.multiple_of(piece * self.rows + chunk * self.size, self.size), self.size)
+
+    def copy(self, way, piece, chunk, source):
+        step = 1 if way == 0 else -1
+        where = self.at(piece, chunk)
+        return pltpu.make_async_remote_copy(
+            src_ref=source.at[where],
+            dst_ref=self.landed.at[way, where],
+            send_sem=self.sent_sem.at[piece, chunk],
+            recv_sem=self.got_sem.at[way, piece, chunk],
+            device_id={"tensor": self.me + step},
+            device_id_type=pl.DeviceIdType.MESH,
+        )
+
+    def edges(self, chunk):
+        last = self.count - 1
+
+        @pl.when(self.me == 0)
+        def _():
+            for piece in range(last, 0, -1):
+                self.copy(0, piece, chunk, self.share).start()
+
+        @pl.when(self.me == last)
+        def _():
+            for piece in range(last):
+                self.copy(1, piece, chunk, self.share).start()
+
+    def relay_one(self, way, piece, chunk):
+        where = self.at(piece, chunk)
+        self.copy(way, piece, chunk, self.stage).wait_recv()
+        self.stage[where] = (
+            self.share[where].astype(jnp.float32) + self.landed[way, where].astype(jnp.float32)
+        ).astype(jnp.bfloat16)
+        self.copy(way, piece, chunk, self.stage).start()
+
+    def relay(self, chunk):
+        last = self.count - 1
+        for piece in range(last, 0, -1):
+            pl.when(jnp.logical_and(self.me > 0, self.me < piece))(
+                functools.partial(self.relay_one, 0, piece, chunk)
+            )
+            other = last - piece
+            pl.when(jnp.logical_and(self.me < last, self.me > other))(
+                functools.partial(self.relay_one, 1, other, chunk)
+            )
+
+    def total(self, chunk, total_ref):
+        where = self.at(self.me, chunk)
+        total_ref[...] = self.share[where].astype(jnp.float32)
+        for way, there in ((0, self.me > 0), (1, self.me < self.count - 1)):
+
+            @pl.when(there)
+            def _(way=way):
+                self.copy(way, self.me, chunk, self.stage).wait_recv()
+                total_ref[...] += self.landed[way, where].astype(jnp.float32)
+
+        return total_ref[...]
+
+    def finish(self, chunk):
+        for piece in range(self.count):
+
+            @pl.when(piece != self.me)
+            def _(piece=piece):
+                self.copy(0, piece, chunk, self.stage).wait_send()
+
+
+class Spread:
+    def __init__(self, count, me, rows, full, sent_sem, got_sem):
+        self.count, self.me, self.rows = count, me, rows
+        self.size = rows // PIECES
+        self.full, self.sent_sem, self.got_sem = full, sent_sem, got_sem
+
+    def at(self, piece, chunk):
+        return pl.ds(pl.multiple_of(piece * self.rows + chunk * self.size, self.size), self.size)
+
+    def copy(self, way, piece, chunk):
+        step = 1 if way == 0 else -1
+        where = self.at(piece, chunk)
+        return pltpu.make_async_remote_copy(
+            src_ref=self.full.at[where],
+            dst_ref=self.full.at[where],
+            send_sem=self.sent_sem.at[way, piece, chunk],
+            recv_sem=self.got_sem.at[piece, chunk],
+            device_id={"tensor": self.me + step},
+            device_id_type=pl.DeviceIdType.MESH,
+        )
+
+    def begin(self, chunk, value):
+        self.full[self.at(self.me, chunk)] = value
+
+        @pl.when(self.me < self.count - 1)
+        def _():
+            self.copy(0, self.me, chunk).start()
+
+        @pl.when(self.me > 0)
+        def _():
+            self.copy(1, self.me, chunk).start()
+
+    def forward_one(self, way, piece, chunk):
+        self.copy(way, piece, chunk).wait_recv()
+
+        @pl.when(self.me < self.count - 1 if way == 0 else self.me > 0)
+        def _():
+            self.copy(way, piece, chunk).start()
+
+    def forward(self, chunk):
+        last = self.count - 1
+        for piece in range(last, -1, -1):
+            pl.when(piece < self.me)(functools.partial(self.forward_one, 0, piece, chunk))
+            other = last - piece
+            pl.when(other > self.me)(functools.partial(self.forward_one, 1, other, chunk))
+
+    def finish(self, chunk):
+        last = self.count - 1
+        for piece in range(self.count):
+
+            @pl.when(jnp.logical_and(piece <= self.me, self.me < last))
+            def _(piece=piece):
+                self.copy(0, piece, chunk).wait_send()
+
+            @pl.when(jnp.logical_and(piece >= self.me, self.me > 0))
+            def _(piece=piece):
+                self.copy(1, piece, chunk).wait_send()
+
+
+def each(body, low=0, high=PIECES):
+    def step(chunk, carry):
+        body(chunk)
+        return carry
+
+    lax.fori_loop(low, high, step, 0)
+
+
+def pipeline(line, spread, final):
+    each(line.edges)
+
+    def step(turn):
+        pl.when(turn < PIECES)(lambda: line.relay(turn))
+        pl.when(jnp.logical_and(turn >= 1, turn <= PIECES))(lambda: final(turn - 1))
+        if spread is not None:
+            pl.when(turn >= 2)(lambda: spread.forward(turn - 2))
+
+    each(step, 0, PIECES + (1 if spread is None else 2))
+    each(line.finish)
+    if spread is not None:
+        each(spread.finish)
+
+
+def own(chunk, rows):
+    size = rows // PIECES
+    return pl.ds(pl.multiple_of(chunk * size, size), size)
+
+
+def forward_kernel(
+    count, share, base, gain, shift, resid, full,
+    stage, landed, total, sent, got, spread_sent, spread_got,
+):
+    me = lax.axis_index("tensor")
+    rows = base.shape[0]
+    greet(count, me)
+    line = Line(count, me, rows, share, stage, landed, sent, got)
+    spread = Spread(count, me, rows, full, spread_sent, spread_got)
+
+    def final(chunk):
+        where = own(chunk, rows)
+        value = base[where] + line.total(chunk, total)
+        resid[where] = value
+        normed, _, _ = layer_norm(value, gain[...], shift[...])
+        spread.begin(chunk, normed.astype(jnp.bfloat16))
+
+    pipeline(line, spread, final)
+
+
+def middle_kernel(
+    count, share, resid, grads, gain, grad_resid, sums, full,
+    stage, landed, total, sent, got, spread_sent, spread_got,
+):
+    me = lax.axis_index("tensor")
+    rows = resid.shape[0]
+    greet(count, me)
+    line = Line(count, me, rows, share, stage, landed, sent, got)
+    spread = Spread(count, me, rows, full, spread_sent, spread_got)
+    sums[...] = jnp.zeros_like(sums)
+
+    def final(chunk):
+        where = own(chunk, rows)
+        grad_two = line.total(chunk, total)
+        _, normed, inv = layer_norm(resid[where], gain[...], gain[...])
+        grad_in, sum_gain, sum_shift = norm_back(grad_two, normed, inv, gain[...])
+        grad_own = grads[where].astype(jnp.float32)
+        value = grad_own + grad_in
+        grad_resid[where] = value
+        spread.begin(chunk, value.astype(jnp.bfloat16))
+        sums[0:1] += sum_gain[None]
+        sums[1:2] += sum_shift[None]
+        sums[2:3] += jnp.sum(value, axis=0, keepdims=True)
+        sums[3:4] += jnp.sum(grad_own, axis=0, keepdims=True)
+
+    pipeline(line, spread, final)
+
+
+def last_kernel(
+    count, share, rows_in, grad_resid, early, gain, d_tokens, sums_out,
+    stage, landed, total, sums, others, sent, got, sum_sent, sum_got,
+):
+    me = lax.axis_index("tensor")
+    rows = rows_in.shape[0]
+    greet(count, me)
+    line = Line(count, me, rows, share, stage, landed, sent, got)
+    sums[...] = early[...]
+
+    def final(chunk):
+        where = own(chunk, rows)
+        grad_one = line.total(chunk, total)
+        _, normed, inv = layer_norm(rows_in[where].astype(jnp.float32), gain[...], gain[...])
+        grad_in, sum_gain, sum_shift = norm_back(grad_one, normed, inv, gain[...])
+        d_tokens[where] = grad_resid[where] + grad_in
+        sums[4:5] += sum_gain[None]
+        sums[5:6] += sum_shift[None]
+
+    pipeline(line, None, final)
+    copies = []
+    for step in range(1, count):
+        copies.append(
+            pltpu.make_async_remote_copy(
+                src_ref=sums,
+                dst_ref=others.at[step],
+                send_sem=sum_sent.at[step],
+                recv_sem=sum_got.at[step],
+                device_id={"tensor": lax.rem(me + step, count)},
+                device_id_type=pl.DeviceIdType.MESH,
+            )
+        )
+    for copy in copies:
+        copy.start()
+    for copy in copies:
+        copy.wait()
+    value = sums[...]
+    for step in range(1, count):
+        value = value + others[step]
+    sums_out[...] = value
+
+
+def call(kernel, ident, count, operands, outs, spreads, sums):
+    length, width = operands[0].shape
+    scratch = [
+        pltpu.VMEM((length, width), jnp.bfloat16),
+        pltpu.VMEM((2, length, width), jnp.bfloat16),
+        pltpu.VMEM((length // count // PIECES, width), jnp.float32),
+    ]
+    if sums:
+        scratch += [
+            pltpu.VMEM((8, width), jnp.float32),
+            pltpu.VMEM((count, 8, width), jnp.float32),
+        ]
+    scratch += [
+        pltpu.SemaphoreType.DMA((count, PIECES)),
+        pltpu.SemaphoreType.DMA((2, count, PIECES)),
+    ]
+    if spreads:
+        scratch += [
+            pltpu.SemaphoreType.DMA((2, count, PIECES)),
+            pltpu.SemaphoreType.DMA((count, PIECES)),
+        ]
+    if sums:
+        scratch += [pltpu.SemaphoreType.DMA((count,)), pltpu.SemaphoreType.DMA((count,))]
+    vmem = pl.BlockSpec(memory_space=pltpu.VMEM)
+    return pl.pallas_call(
+        functools.partial(kernel, count),
+        out_shape=[jax.ShapeDtypeStruct(shape, dtype) for shape, dtype in outs],
+        in_specs=[vmem] * len(operands),
+        out_specs=[vmem] * len(outs),
+        scratch_shapes=scratch,
+        compiler_params=pltpu.CompilerParams(
+            collective_id=ident, has_side_effects=True, vmem_limit_bytes=24 << 20
+        ),
+        cost_estimate=pl.CostEstimate(
+            flops=length * width * 20, bytes_accessed=length * width * 64, transcendentals=0
+        ),
+    )(*operands)
 
 
 def local(
@@ -120,16 +428,22 @@
     attn_probs = jnp.exp(scores - log_total).astype(jnp.bfloat16)
     context = jnp.einsum("hqk,khe->qhe", attn_probs, values_all, preferred_element_type=jnp.float32)
     context = context.astype(jnp.bfloat16).reshape(length, head_count * head_size)
-    attn_share = lax.psum_scatter(
-        jnp.dot(context, w_dense, preferred_element_type=jnp.float32),
-        "tensor",
-        scatter_dimension=0,
-        tiled=True,
-    )
-    tokens_share = lax.dynamic_slice_in_dim(tokens_f, offset, share_rows, 0)
-    resid_one = tokens_share + attn_share + b_dense
-    norm_two, normed_two, inv_two = layer_norm(resid_one, ln2_gain, ln2_bias)
-    input_two = lax.all_gather(norm_two.astype(jnp.bfloat16), "tensor", axis=0, tiled=True)
+    width = tokens.shape[1]
+    own_tokens = lax.dynamic_slice_in_dim(tokens, offset, share_rows, 0)
+    resid_one, input_two = call(
+        forward_kernel,
+        1,
+        tensor_count,
+        (
+            jnp.dot(context, w_dense, preferred_element_type=jnp.float32).astype(jnp.bfloat16),
+            own_tokens.astype(jnp.float32) + b_dense,
+            ln2_gain[None],
+            ln2_bias[None],
+        ),
+        (((share_rows, width), jnp.float32), ((length, width), jnp.bfloat16)),
+        True,
+        False,
+    )
     pre_act = jnp.dot(input_two, w_fc1, preferred_element_type=jnp.float32) + b_fc1.reshape(-1)
     hidden = gelu_value(pre_act).astype(jnp.bfloat16)
     mlp_share = lax.psum_scatter(
@@ -139,20 +453,30 @@
         tiled=True,
     ).astype(jnp.float32)
     block_out = (resid_one + mlp_share + b_fc2).astype(jnp.bfloat16)
-    grad_share = lax.dynamic_slice_in_dim(cotangent, offset, share_rows, 0).astype(jnp.float32)
-    g_b_fc2 = jnp.sum(grad_share, axis=0)
+    grad_share = lax.dynamic_slice_in_dim(cotangent, offset, share_rows, 0)
     g_w_fc2 = cross_rows(hidden, cotangent)
     grad_pre = dot_transposed(cotangent, w_fc2) * gelu_slope(pre_act)
     g_b_fc1 = jnp.sum(grad_pre, axis=0).reshape(b_fc1.shape)
     grad_pre_b = grad_pre.astype(jnp.bfloat16)
     g_w_fc1 = cross_rows(input_two, grad_pre_b)
-    grad_two = lax.psum_scatter(
-        dot_transposed(grad_pre_b, w_fc1), "tensor", scatter_dimension=0, tiled=True
-    )
-    grad_ln_two, g_ln2_gain, g_ln2_bias = norm_back(grad_two, normed_two, inv_two, ln2_gain)
-    grad_resid = grad_share + grad_ln_two
-    g_b_dense = jnp.sum(grad_resid, axis=0)
-    grad_resid_b = lax.all_gather(grad_resid.astype(jnp.bfloat16), "tensor", axis=0, tiled=True)
+    grad_resid, sums_two, grad_resid_b = call(
+        middle_kernel,
+        2,
+        tensor_count,
+        (
+            dot_transposed(grad_pre_b, w_fc1).astype(jnp.bfloat16),
+            resid_one,
+            grad_share,
+            ln2_gain[None],
+        ),
+        (
+            ((share_rows, width), jnp.float32),
+            ((8, width), jnp.float32),
+            ((length, width), jnp.bfloat16),
+        ),
+        True,
+        False,
+    )
     g_w_dense = cross_rows(context, grad_resid_b)
     grad_context = dot_transposed(grad_resid_b, w_dense).reshape(length, head_count, head_size)
     delta = jnp.einsum(
@@ -187,31 +511,57 @@
         .reshape(length, 3 * head_count * head_size)
     )
     g_w_qkv = cross_rows(input_one, grad_qkv)
-    grad_one = lax.psum_scatter(
-        dot_transposed(grad_qkv, w_qkv).astype(jnp.bfloat16),
-        "tensor",
-        scatter_dimension=0,
-        tiled=True,
-    ).astype(jnp.float32)
-    normed_share = lax.dynamic_slice_in_dim(normed_one, offset, share_rows, 0)
-    inv_share = lax.dynamic_slice_in_dim(inv_one, offset, share_rows, 0)
-    grad_ln_one, g_ln1_gain, g_ln1_bias = norm_back(grad_one, normed_share, inv_share, ln1_gain)
-    d_tokens = grad_resid + grad_ln_one
-    sent_qkv, sent_qv, sent_dense, sent_fc1, sent_bias, sent_fc2 = (
-        lax.psum_scatter(g_w_qkv, "dp", scatter_dimension=0, tiled=True),
-        lax.psum_scatter(g_b_qv, "dp", scatter_dimension=1, tiled=True),
-        lax.psum_scatter(g_w_dense, "dp", scatter_dimension=1, tiled=True),
-        lax.psum_scatter(g_w_fc1, "dp", scatter_dimension=0, tiled=True),
-        lax.psum_scatter(g_b_fc1, "dp", scatter_dimension=1, tiled=True),
-        lax.psum_scatter(g_w_fc2, "dp", scatter_dimension=1, tiled=True),
-    )
+    d_tokens, sums_all = call(
+        last_kernel,
+        3,
+        tensor_count,
+        (
+            dot_transposed(grad_qkv, w_qkv).astype(jnp.bfloat16),
+            own_tokens,
+            grad_resid,
+            sums_two,
+            ln1_gain[None],
+        ),
+        (((share_rows, width), jnp.float32), ((8, width), jnp.float32)),
+        False,
+        True,
+    )
+    dp_count = lax.axis_size("dp")
+
+    def scatter(grad, dim):
+        return lax.psum_scatter(
+            grad.astype(jnp.bfloat16), "dp", scatter_dimension=dim, tiled=True
+        ).astype(jnp.float32)
+
+    sent_fc2 = scatter(g_w_fc2, 1)
+    sent_fc1 = scatter(g_w_fc1, 0)
+    sent_dense = scatter(g_w_dense, 1)
+    sent_qkv = scatter(g_w_qkv, 0)
+    split = width // (dp_count * tensor_count)
+    gains = lax.dynamic_index_in_dim(
+        sums_all[:6].reshape(6, dp_count, tensor_count, split), tensor_rank, 2, keepdims=False
+    )
+    qv_rows, qv_cols = g_b_qv.shape[0], g_b_qv.shape[1] // dp_count
+    up_rows, up_cols = g_b_fc1.shape[0], g_b_fc1.shape[1] // dp_count
+    packed = jnp.concatenate(
+        [
+            jnp.moveaxis(gains, 1, 0).reshape(dp_count, -1),
+            jnp.moveaxis(g_b_qv.reshape(qv_rows, dp_count, qv_cols), 1, 0).reshape(dp_count, -1),
+            jnp.moveaxis(g_b_fc1.reshape(up_rows, dp_count, up_cols), 1, 0).reshape(dp_count, -1),
+        ],
+        axis=1,
+    )
+    small = lax.psum_scatter(packed, "dp", scatter_dimension=0, tiled=True)[0]
+    gain_sums = small[: 6 * split].reshape(6, split)
+    sent_qv = small[6 * split : 6 * split + qv_rows * qv_cols].reshape(qv_rows, qv_cols)
+    sent_bias = small[6 * split + qv_rows * qv_cols :].reshape(up_rows, up_cols)
     small_sums = (
-        lax.psum_scatter(g_ln1_gain, ("dp", "tensor"), scatter_dimension=0, tiled=True),
-        lax.psum_scatter(g_ln1_bias, ("dp", "tensor"), scatter_dimension=0, tiled=True),
-        lax.psum_scatter(g_b_dense, ("dp", "tensor"), scatter_dimension=0, tiled=True),
-        lax.psum_scatter(g_ln2_gain, ("dp", "tensor"), scatter_dimension=0, tiled=True),
-        lax.psum_scatter(g_ln2_bias, ("dp", "tensor"), scatter_dimension=0, tiled=True),
-        lax.psum_scatter(g_b_fc2, ("dp", "tensor"), scatter_dimension=0, tiled=True),
+        gain_sums[4],
+        gain_sums[5],
+        gain_sums[2],
+        gain_sums[0],
+        gain_sums[1],
+        gain_sums[3],
     )
     return (
         block_out,

time: 522 us -> 380 us (0.73)
  waiting for transfers between devices: 381 us -> 76.6 us
  Pallas kernels: 0 us -> 191 us
  blocking collectives: 39.4 us -> 22.6 us
  matrix products: 50.1 us -> 40.7 us
  other arithmetic: 18.9 us -> 11.9 us
    reduce_scatter x7 -> x2, waiting for transfers between devices: 264 us -> 42.3 us  [scatter(): lax.psum_scatter(grad.astype(jnp.bfloat16), 'dp', scatter_dimension=dim,...]
    pallas_call x0 -> x3, Pallas kernels: none -> 191 us  [call(): pl.pallas_call(functools.partial(kernel, count), out_shape=[jax.ShapeDtyp...]
    all_gather x2 -> x0, waiting for transfers between devices: 53.1 us -> none  [the longest x1 27.3 us: local(): lax.all_gather(norm_two.astype(jnp.bfloat16), 'tensor', axis=0, tiled=True)]
    reduce_scatter x1, waiting for transfers between devices: 27.2 us -> 0.01 us  [local(): lax.psum_scatter(jnp.dot(hidden, w_fc2, preferred_element_type=jnp.float3...]
    unnamed x1, blocking collectives: 39.4 us -> 22.6 us
    unnamed x14 -> x7, waiting for transfers between devices: 36.6 us -> 34.2 us
    unnamed x52 -> x62, local copies, waits for them, and re-layouts: 11.9 us -> 14.2 us
  transfers between devices with their start and end apart: 12 -> 5, of which waited for: 12 -> 2; matrix products, arithmetic and copies ran while one was open for 10% -> 11% of each run, Pallas kernels for 0% -> 13%
where the time goes in v1:
time: 380 us; the launch traced here: 379 us
  Pallas kernels  191 us (50%)
  waiting for transfers between devices  76.6 us (20%)
  matrix products  40.7 us (11%)
  blocking collectives  22.6 us (6%)
  local copies, waits for them, and re-layouts  21.6 us (6%)
  between operations  14.3 us (4%)
  other arithmetic  11.9 us (3%)
    pallas_call x3, Pallas kernels, call(): pl.pallas_call(functools.partial(kernel, count), out_shape=[jax.ShapeDtyp...  191 us
    reduce_scatter x2, waiting for transfers between devices, scatter(): lax.psum_scatter(grad.astype(jnp.bfloat16), 'dp', scatter_dimension=dim,...  42.3 us
    unnamed x7, waiting for transfers between devices  34.2 us
    unnamed x1, blocking collectives  22.6 us
    unnamed x62, local copies, waits for them, and re-layouts  14.2 us
    dot_general x4, matrix products, cross_rows(): lax.dot_general(left_mat, right_mat, (((0,), (0,)), ((), ())), preferred_...  12.6 us
    dot_general x4, matrix products, dot_transposed(): lax.dot_general(left_mat, right_mat, (((1,), (1,)), ((), ())), preferred_...  8.45 us
  transfers between devices with their start and end apart: 5, of which 2 were waited for; matrix products, arithmetic and copies ran while one was open for 11% of the time, Pallas kernels for 13%

profile of v1, /device:TPU:0, one launch (start us, length us, event | category | flops | bytes accessed | tf_op | source)
XLA Modules:
  0.0 378.8 jit_solution(13048702525845904086)
XLA Ops:
  7.3 1.1 subtract_convert_fusion
  8.4 1.5 convert_reduce_fusion
  9.9 0.4 fusion.3
  10.4 0.1 pad.9.clone
  10.5 0.1 add.121
  10.6 3.8 %add_convert_fusion = bf16[512,768]{1,0:T(8,128)(2,1)} fusion(bf16[1024,768]{1,0:T(8,128)(2,1)} %param.19, f32[768]{0:T(1024)S(1)} %add.121, bf16[512,1024]{1,0:T(8,128)(2,1)} %param.15, f32[1024]{0:T(1024)S(1)} %copy-done.23, f32[1024]{0:T(1024)S(1)} %copy-done.6, f32[512]{0:T(512)S(1)} %add_rsqrt_fusion, f32[512]{0:T(512)S(1)} %broadcast_multiply_fusion), kind=kOutput, calls=%fused_computation.25 | convolution fusion | flops 809238528 | bytes 3423232 | tf_op jit(solution)/shard_map/dot_general | solution.py:418
  14.4 1.4 copy.51
  15.8 0.2 fusion.16
  16.0 2.6 fusion.28
  18.6 0.6 exponential_reduce_fusion
  19.3 1.3 copy-done.8
  20.6 0.8 convolution_convert_fusion.8
  21.4 1.1 convert_add_fusion
  22.5 1.1 constant_dynamic-slice_fusion.1.grads
  23.6 1.5 convolution_convert_fusion.6.share
  25.2 73.3 %shard_map.254 = (f32[128,1024]{1,0:T(8,128)S(1)}, bf16[512,1024]{1,0:T(8,128)(2,1)S(1)}) custom-call(bf16[512,1024]{1,0:T(8,128)(2,1)S(1)} %convolution_convert_fusion.6.share, f32[128,1024]{1,0:T(8,128)S(1)} %get-tuple-element.28.base, f32[1,1024]{1,0:T(1,128)S(1)} %bitcast.105, f32[1,1024]{1,0:T(1,128)S(1)} %bitcast.107), custom_call_target="tpu_custom_call" | custom-call | flops 10485760 | bytes 33554432 | tf_op jit(solution)/shard_map/pallas_call | solution.py:374
  98.6 1.3 fusion.30
  99.9 0.3 copy-done.17
  100.1 2.4 fusion.29
  102.6 1.3 convolution_convert_fusion.4.share
  103.9 68.5 %shard_map.255 = (f32[128,1024]{1,0:T(8,128)S(1)}, f32[8,1024]{1,0:T(8,128)S(1)}, bf16[512,1024]{1,0:T(8,128)(2,1)S(1)}) custom-call(bf16[512,1024]{1,0:T(8,128)(2,1)S(1)} %convolution_convert_fusion.4.share, f32[128,1024]{1,0:T(8,128)S(1)} %get-tuple-element.21.resid, bf16[128,1024]{1,0:T(8,128)(2,1)S(1)} %constant_dynamic-slice_fusion.1.grads, ...), custom_call_target="tpu_custom_call" | custom-call | flops 10485760 | bytes 33554432 | tf_op jit(solution)/shard_map/pallas_call | solution.py:374
  172.4 1.0 copy-done.1
  173.4 1.2 convolution_convert_fusion.7
  174.7 2.0 copy.76
  176.7 0.2 reduce-scatter.10.cloned.1.call-start
  177.0 4.2 %convolution_convert_fusion.5 = bf16[512,1024]{1,0:T(8,128)(2,1)} fusion(bf16[1024,1024]{1,0:T(8,128)(2,1)S(1)} %copy-done, f32[512,1024]{1,0:T(8,128)} %copy-done.26, f32[1024]{0:T(1024)S(1)} %bitcast.129), kind=kOutput, calls=%fused_computation.28 | convolution fusion | flops 1079508992 | bytes 5246976 | tf_op jit(solution)/shard_map/dot_general | solution.py:450
  181.2 2.0 multiply_reduce_fusion
  183.3 3.4 multiply_convert_fusion
  186.7 0.8 fusion.15
  187.4 0.8 convolution_bitcast_fusion
  188.2 0.6 fusion.25
  188.8 0.1 pad_maximum_fusion
  188.9 0.1 copy.60
  189.0 0.9 copy-done.16
  189.9 0.4 copy-done.11
  190.3 2.5 convolution_convert_fusion.2
  192.8 4.8 %convolution_convert_fusion = bf16[1024,1024]{1,0:T(8,128)(2,1)} fusion(bf16[512,1024]{1,0:T(8,128)(2,1)} %param.29, f32[512,1024]{1,0:T(8,128)} %copy-done.26, f32[1024]{0:T(1024)S(1)} %bitcast.130), kind=kOutput, calls=%fused_computation.22 | convolution fusion | flops 1080033280 | bytes 5246976 | tf_op jit(solution)/shard_map/dot_general | solution.py:62
  197.6 3.9 %copy.78 = bf16[1024,1024]{0,1:T(8,128)(2,1)} copy(bf16[1024,1024]{1,0:T(8,128)(2,1)} %convolution_convert_fusion) | data formatting | bytes 4194304
  201.6 4.1 %convolution_convert_fusion.1 = bf16[1024,1024]{1,0:T(8,128)(2,1)} fusion(bf16[512,1024]{1,0:T(8,128)(2,1)} %copy-done.7, bf16[512,1024]{1,0:T(8,128)(2,1)} %copy-done.27), kind=kOutput, calls=%fused_computation.23 | convolution fusion | flops 1074790400 | bytes 4194304 | tf_op jit(solution)/shard_map/dot_general | solution.py:62
  205.8 0.1 pad_maximum_fusion.3
  205.9 0.1 reshape.177
  206.0 0.1 reshape.178
  206.0 2.7 convolution_convert_fusion.3.share
  208.8 48.9 %shard_map.256 = (f32[128,1024]{1,0:T(8,128)S(1)}, f32[8,1024]{1,0:T(8,128)S(1)}) custom-call(bf16[512,1024]{1,0:T(8,128)(2,1)S(1)} %convolution_convert_fusion.3.share, bf16[128,1024]{1,0:T(8,128)(2,1)S(1)} %get-tuple-element.29.rows_in, f32[128,1024]{1,0:T(8,128)S(1)} %get-tuple-element.24.grad_resid, f32[8,1024]{1,0:T(8,128)S(1)} %get-tuple-element.25.early, ...), custom_call_target="tpu_custom_call" | custom-call | flops 10485760 | bytes 33554432 | tf_op jit(solution)/shard_map/pallas_call | solution.py:374
  257.7 0.8 copy-done.2
  258.5 0.1 reshape.175
  258.8 0.1 reshape.179
  258.9 0.6 dynamic-slice
  259.5 22.6 %all-reduce = f32[8,384]{1,0:T(8,128)S(1)} all-reduce(f32[8,384]{1,0:T(8,128)S(1)} %pad_maximum_fusion.1), channel_id=3, replica_groups=mesh['dp'=8,'tensor'=4] {'dp'}, use_global_device_ids=true, to_apply=%region_8.9.clone | all-reduce | flops 3072 | bytes 24576
  282.1 0.7 dynamic-slice_reduce_fusion
  282.9 0.7 reshape.181
  283.6 0.7 dynamic-slice_reduce_fusion.1
  284.3 0.7 reshape.180
  285.0 1.3 dynamic-slice_bitcast_fusion
  286.2 0.9 copy.77
  287.2 0.7 convert_element_type.120
  287.9 1.7 add_convert_fusion.1
  289.6 1.7 convert_element_type.118
  291.3 34.2 %reduce-scatter.18.cloned.1.call-done = bf16[128,1024]{1,0:T(8,128)(2,1)} async-done(((bf16[1024,1024]{1,0:T(8,128)(2,1)}), bf16[128,1024]{1,0:T(8,128)(2,1)}) %reduce-scatter.18.cloned.1.call-update) | async-done | bytes 262160
  325.4 1.1 copy.79
  326.6 0.8 convert_element_type.124
  327.4 42.3 %reduce-scatter.14.cloned.1.call-done = bf16[128,1024]{1,0:T(8,128)(2,1)} async-done(((bf16[1024,1024]{1,0:T(8,128)(2,1)}), bf16[128,1024]{1,0:T(8,128)(2,1)}) %reduce-scatter.14.cloned.1.call-update) | async-done | bytes 262160 | tf_op jit(solution)/shard_map/reduce_scatter | solution.py:532
  369.7 1.8 convert_element_type.122
  371.5 0.8 copy.85
  (76 shorter events, 0.8 us)
Async XLA Ops:
  7.2 92.7 %copy-start = (bf16[1024,1024]{1,0:T(8,128)(2,1)S(1)}, bf16[1024,1024]{1,0:T(8,128)(2,1)}, u32[]{:S(2)}) copy-start(bf16[1024,1024]{1,0:T(8,128)(2,1)} %param.27) | copy-start | bytes 6291460
  7.2 3.1 copy-start.19
  7.2 3.4 copy-start.6
  7.2 3.4 copy-start.23
  7.2 279.0 %reduce-scatter.16.cloned.1.call-start = ((), (), s32[]{:S(2)}) async-start(), calls=%async_computation.8 | async-start | bytes 589824
  7.3 2.6 copy-start.10
  10.6 5.2 %copy-start.18 = (s32[1,512]{1,0:T(1,128)S(1)}, s32[1,512]{1,0:T(1,128)}, u32[]{:S(2)}) copy-start(s32[1,512]{1,0:T(1,128)} %param.16) | copy-start | bytes 6148
  15.8 3.5 copy-start.12
  18.6 1.9 copy-start.8
  20.6 0.8 copy-start.20
  21.3 3.8 %copy-start.14 = (bf16[4,64,512]{2,1,0:T(8,128)(2,1)}, bf16[4,64,512]{2,1,0:T(8,128)(2,1)S(1)}, u32[]{:S(2)}) copy-start(bf16[4,64,512]{2,1,0:T(8,128)(2,1)S(1)} %convolution_convert_fusion.8) | copy-start | bytes 786436
  21.4 3.8 %copy-start.4 = (f32[1024]{0:T(1024)S(1)}, f32[1024]{0:T(1024)}, u32[]{:S(2)}) copy-start(f32[1024]{0:T(1024)} %param.23) | copy-start | bytes 12292
  21.4 3.8 %copy-start.5 = (f32[1024]{0:T(1024)S(1)}, f32[1024]{0:T(1024)}, u32[]{:S(2)}) copy-start(f32[1024]{0:T(1024)} %param.24) | copy-start | bytes 12292
  22.5 76.0 %copy-start.22 = (bf16[1024,1024]{1,0:T(8,128)(2,1)S(1)}, bf16[1024,1024]{1,0:T(8,128)(2,1)}, u32[]{:S(2)}) copy-start(bf16[1024,1024]{1,0:T(8,128)(2,1)} %param.25) | copy-start | bytes 6291460
  98.5 1.3 copy-start.7
  98.5 1.6 copy-start.17
  98.6 1.6 copy-start.24
  99.8 2.7 copy-start.26
  102.6 1.3 copy-start.27
  102.6 70.8 %copy-start.15 = (bf16[4,64,512]{2,1,0:T(8,128)(2,1)S(1)}, bf16[4,64,512]{2,1,0:T(8,128)(2,1)}, u32[]{:S(2)}) copy-start(bf16[4,64,512]{2,1,0:T(8,128)(2,1)} %copy-done.14) | copy-start | bytes 786436
  172.4 1.0 copy-start.1
  176.7 111.1 %reduce-scatter.10.cloned.1.call-start = ((), (), s32[]{:S(2)}) async-start(), calls=%async_computation.5 | async-start | bytes 1310720 | tf_op jit(solution)/shard_map/reduce_scatter | solution.py:449
  181.1 108.4 %reduce-scatter.12.cloned.1.call-start = ((), (), s32[]{:S(2)}) async-start(), calls=%async_computation.6 | async-start | bytes 1769472 | tf_op jit(solution)/shard_map/reduce_scatter | solution.py:532
  181.2 2.0 copy-start.13
  183.2 4.2 %copy-start.9 = (f32[4,512,512]{1,2,0:T(8,128)S(1)}, f32[4,512,512]{1,2,0:T(8,128)}, u32[]{:S(2)}) copy-start(f32[4,512,512]{1,2,0:T(8,128)} %copy-done.8) | copy-start | bytes 12582916
  188.8 1.5 copy-start.11
  189.0 0.9 copy-start.16
  192.8 132.7 %reduce-scatter.18.cloned.1.call-start = ((), (), s32[]{:S(2)}) async-start(), calls=%async_computation.9 | async-start | bytes 2359296
  201.6 168.2 %reduce-scatter.14.cloned.1.call-start = ((), (), s32[]{:S(2)}) async-start(), calls=%async_computation.7 | async-start | bytes 2359296 | tf_op jit(solution)/shard_map/reduce_scatter | solution.py:532
  208.7 50.1 %copy-start.25 = (u32[32]{0:T(128)S(1)}, u32[32]{0:T(128)}, u32[]{:S(2)}) copy-start(u32[32]{0:T(128)} %constant.54) | copy-start | bytes 388
  208.8 79.1 %copy-start.21 = (f32[1024]{0:T(1024)S(1)}, f32[1024]{0:T(1024)}, u32[]{:S(2)}) copy-start(f32[1024]{0:T(1024)} %param.28) | copy-start | bytes 12292
  257.7 0.8 copy-start.2
  258.9 112.7 %copy-start.3 = (f32[128,1024]{1,0:T(8,128)S(1)}, f32[128,1024]{1,0:T(8,128)}, u32[]{:S(2)}) copy-start(f32[128,1024]{1,0:T(8,128)} %copy-done.2) | copy-start | bytes 1572868
Sparse Core Ops, SparseCore 0:
  176.8 32.3 reduce-scatter.15
  211.5 28.3 reduce-scatter.9
  243.2 37.9 reduce-scatter.11
  284.3 41.0 reduce-scatter.17
  328.6 41.1 reduce-scatter.13
